TPU v7x, 128 devices: a whole 4x4x4 slice. The times are simulated.
128 devices in a mesh: bin: 8 (over y, core), col: 16 (over z, x).
Axes of the slice: x: 4, y: 4, z: 4, core: 2. Of those that a mesh axis runs over, the one named last changes fastest.
Arguments:
- les_source: float32 [128, 106, 16384], P('bin', None, 'col'), may hold values from -6 to 6
- cell_owner: int32 [16384, 1], P('col'), may hold values from 0 to 15; in each aligned block of 1024 rows (0 to 1023, 1024 to 2047, ...) at most 128 rows name the same one
- cell_slot: int32 [16384], P('col'), may hold values from 0 to 127
- pdf_weight: float32 [128, 16384], P('bin', 'col'), may hold values from 0.02 to 0.2
- prior_state: float32 [128, 106, 2048], P('bin', None, 'col'), may hold values from -24 to 24
- dissip: float32 [2048], P('col'), may hold values from 500 to 5000
- react_inverse: float32 [128, 106, 106], P('bin'), may hold values from -0.625 to 0.625
Outputs:
- new_state: float32 [128, 106, 2048], P('bin', None, 'col')
- les_species: float32 [106, 16384], P(None, 'col')
Inputs may be any that keep to these rules, and one draw needn't show every extreme that they name: `cell_owner`: among the 1024 cells of one device at most 128 have any one owner, and exactly 128 cells of some device share one owner.
All inputs are finite; a program needn't handle non-finite values.
Results may differ from a plain program's by a relative error of at most 0.00015.
Values sent between devices are 32-bit elements; how exact they have to be, the bound alone decides.
A program may use at most 128 MiB of HBM per device.

v0:
```python
import jax
import jax.numpy as jnp
from jax import lax
from jax.sharding import PartitionSpec as P

highest = lax.Precision.HIGHEST


def prefix(array, axis, combine, identity, reverse):
    count, place = (lax.axis_size(axis), lax.axis_index(axis))
    everything = jax.tree.map(lambda part: lax.all_gather(part, axis), array)
    start = jax.tree.map(
        lambda part, zero: jnp.broadcast_to(jnp.asarray(zero, part.dtype), part.shape),
        array,
        identity,
    )

    def turn(k, before):
        at = count - 1 - k if reverse else k
        reached = at > place if reverse else at < place
        new = combine(before, jax.tree.map(lambda part: part[at], everything))
        return jax.tree.map(lambda a, b: jnp.where(reached, a, b), new, before)

    return lax.fori_loop(0, count, turn, start)


def mixing_profile(count):
    centre = (jnp.arange(count, dtype=jnp.float32) + 0.5) / count
    return 4.0 * centre * (1.0 - centre) + 0.05


def compose_affine(earlier_map, later_map):
    return (earlier_map[0] * later_map[0], later_map[0] * earlier_map[1] + later_map[1])


def pivot_chain(coeffs):

    def advance(ratio_earlier, diffusion):
        pivot_current = 1.0 + 2.0 * diffusion - diffusion * ratio_earlier
        ratio_current = diffusion / pivot_current
        return (ratio_current, (ratio_current, pivot_current))

    unused_item, (ratio_values, pivot_values) = lax.scan(
        advance, jnp.zeros(coeffs.shape[1:], jnp.float32), coeffs
    )
    return (ratio_values, pivot_values)


def bin_solve(right_hand_side, dissip):
    local_bins = right_hand_side.shape[0]
    bin_count = local_bins * lax.axis_size("bin")
    coeffs = mixing_profile(bin_count)[:, None] * dissip[None, :]
    ratios_all, pivots_all = pivot_chain(coeffs)
    first_bin = lax.axis_index("bin") * local_bins
    ratio_values = lax.dynamic_slice_in_dim(ratios_all, first_bin, local_bins, 0)
    pivot_values = lax.dynamic_slice_in_dim(pivots_all, first_bin, local_bins, 0)
    zeroed_plane = jnp.zeros(right_hand_side.shape[1:], jnp.float32)
    identity_line = jnp.ones(right_hand_side.shape[2:], jnp.float32)

    def eliminate_step(previous, sweep_inputs):
        ratio_current, pivot_current, source_term = sweep_inputs
        current_entry = source_term / pivot_current[None, :] + ratio_current[None, :] * previous
        return (current_entry, current_entry)

    unused_item, partial_elimination = lax.scan(
        eliminate_step, zeroed_plane, (ratio_values, pivot_values, right_hand_side)
    )
    growth_factor = jnp.cumprod(ratio_values, axis=0)
    unused_item, incoming_entry = prefix(
        (growth_factor[-1], partial_elimination[-1]),
        "bin",
        compose_affine,
        (identity_line, zeroed_plane),
        False,
    )
    eliminated_rows = partial_elimination + growth_factor[:, None, :] * incoming_entry[None]

    def substitute(following_entry, sweep_inputs):
        ratio_current, elimination_value = sweep_inputs
        current_entry = elimination_value + ratio_current[None, :] * following_entry
        return (current_entry, current_entry)

    unused_item, partial_back = lax.scan(
        substitute, zeroed_plane, (ratio_values, eliminated_rows), reverse=True
    )
    decay_back = jnp.cumprod(ratio_values[::-1], axis=0)[::-1]
    unused_item, outgoing = prefix(
        (decay_back[0], partial_back[0]), "bin", compose_affine, (identity_line, zeroed_plane), True
    )
    return partial_back + decay_back[:, None, :] * outgoing[None]


def contract_last(left_mat, right_mat):
    return lax.dot_general(left_mat, right_mat, (((1,), (1,)), ((), ())), precision=highest)


def local(les_source, cell_owner, cell_slot, pdf_weight, prior_state, dissip, react_inverse):
    local_bins, species, cell_num = les_source.shape
    col_local = prior_state.shape[2]
    groups = lax.axis_size("col")
    flat_source = les_source.reshape(local_bins * species, cell_num)
    column = cell_owner[:, 0] * col_local + cell_slot
    all_cols = col_local * groups
    member = (column[:, None] == jnp.arange(all_cols, dtype=jnp.int32)[None, :]).astype(jnp.float32)
    col_terms = jnp.dot(flat_source, member, precision=highest).reshape(
        local_bins, species, all_cols
    )
    cond_source = lax.psum_scatter(col_terms, "col", scatter_dimension=2, tiled=True)
    right_hand_side = prior_state + cond_source
    solved_values = bin_solve(right_hand_side, dissip)
    new_state = jnp.einsum("ist,itc->isc", react_inverse, solved_values, precision=highest)
    portion = lax.all_gather(new_state, "col", axis=2, tiled=True)
    span_cols = portion.shape[2]
    chosen = (column[:, None] == jnp.arange(span_cols, dtype=jnp.int32)[None, :]).astype(
        jnp.float32
    )
    picked = contract_last(portion.reshape(local_bins * species, span_cols), chosen)
    at_cells = jnp.zeros((local_bins, species, cell_num), jnp.float32) + picked.reshape(
        local_bins, species, cell_num
    )
    partial_species = jnp.einsum("il,isl->sl", pdf_weight, at_cells, precision=highest)
    les_species = lax.psum(partial_species, "bin")
    return (new_state, les_species)


def solution(mesh):
    placed = (
        P("bin", None, "col"),
        P("col", None),
        P("col"),
        P("bin", "col"),
        P("bin", None, "col"),
        P("col"),
        P("bin", None, None),
    )
    return jax.shard_map(
        local,
        mesh=mesh,
        in_specs=placed,
        out_specs=(P("bin", None, "col"), P(None, "col")),
        check_vma=False,
    )
```

profile of v0, /device:TPU:1, one launch (start us, length us, event | category | flops | bytes accessed | tf_op | source)
XLA Modules:
  0.0 405.1 jit_solution(4831074687814479184)
XLA Ops:
  7.2 0.0 copy-start
  7.2 0.0 reduce-scatter.2.cloned.1.call-start
  7.2 0.8 broadcast_multiply_fusion.1
  8.0 9.9 %copy.16 = f32[16,106,1024]{2,1,0:T(8,128)} copy(f32[16,106,1024]{2,0,1:T(8,128)} %param.17) | data formatting | bytes 13893632 | tf_op args[0]
  17.9 0.0 copy-start.3
  17.9 6.6 %reshape.31 = f32[1696,1024]{1,0:T(8,128)} reshape(f32[16,106,1024]{2,1,0:T(8,128)} %copy.16) | data formatting | bytes 13893632 | tf_op jit(solution)/shard_map/reshape | solution.py:101
  24.6 0.0 copy-done.3
  24.6 27.6 %convolution_bitcast_fusion = f32[1696,2048]{1,0:T(8,128)} fusion(f32[1696,1024]{1,0:T(8,128)} %reshape.31, s32[1024]{0:T(1024)S(1)} %add.147), kind=kOutput, calls=%fused_computation.26 | convolution fusion | flops 42683334656 | bytes 20844544 | tf_op jit(solution)/shard_map/dot_general | solution.py:105
  52.1 10.4 %reshape.32 = f32[16,106,2048]{2,1,0:T(8,128)} reshape(f32[1696,2048]{1,0:T(8,128)} %convolution_bitcast_fusion) | data formatting | bytes 27787264 | tf_op jit(solution)/shard_map/reshape | solution.py:105
  62.5 0.0 copy-start.4
  62.5 0.0 copy-start.2
  62.5 0.0 reduce-scatter.2.cloned.1.call-update
  62.6 0.0 all-gather.4.cloned.1.call-start
  62.7 0.5 copy-done.4
  63.2 0.1 broadcast_multiply_fusion
  63.3 14.4 %while.75 = (s32[]{:T(128)}, f32[128]{0:T(128)S(1)}, f32[128,128]{1,0:T(8,128)S(1)}, f32[128,128]{1,0:T(8,128)S(1)}, f32[128,128]{1,0:T(8,128)S(1)}, /*index=5*/s32[]{:T(128)}, s32[]{:T(128)}) while((s32[]{:T(128)}, f32[128]{0:T(128)S(1)}, f32[128,128]{1,0:T(8,128)S(1)}, f32[128,128]{1,0:T(8,128)S(1)}, f32[128,128]{1,0:T(8,128)S(1)}, ...), condition=%wide.region_1.2_spmd.clone, body=%wide.region_0.0_spmd.clone.sunk | while | flops 771 | bytes 4195 | solution.py:43
  77.8 12.0 %all-gather = f32[8,1,128]{2,1,0:T(1,128)S(1)} all-gather(f32[1,1,128]{2,1,0:T(1,128)S(1)} %slice_bitcast_fusion.1), channel_id=1, replica_groups=mesh['bin'=8,'col'=16] {'bin'}, dimensions={0}, use_global_device_ids=true | all-gather | bytes 4608 | tf_op jit(solution)/shard_map/all_gather | solution.py:11
  89.9 8.2 %all-gather.1 = f32[8,1,128]{2,1,0:T(1,128)S(1)} all-gather(f32[1,1,128]{2,1,0:T(1,128)S(1)} %slice_bitcast_fusion), channel_id=1, replica_groups=mesh['bin'=8,'col'=16] {'bin'}, dimensions={0}, use_global_device_ids=true | all-gather | bytes 4608 | tf_op jit(solution)/shard_map/all_gather | solution.py:11
  98.1 69.3 %reduce-scatter.2.cloned.1.call-done = f32[16,106,128]{2,1,0:T(8,128)} async-done(((f32[16,106,2048]{2,1,0:T(8,128)}), f32[16,106,128]{2,1,0:T(8,128)}) %reduce-scatter.2.cloned.1.call-update) | async-done | bytes 868368 | tf_op jit(solution)/shard_map/reduce_scatter | solution.py:108
  167.3 0.0 copy-done.2
  167.3 1.5 copy_add_fusion
  168.8 0.0 copy-start.5
  168.8 0.1 broadcast.45.clone
  168.9 1.0 while.76
  169.9 14.1 %all_gather.16 = f32[8,106,128]{2,1,0:T(8,128)S(1)} all-gather(f32[1,106,128]{2,1,0:T(8,128)S(1)} %slice.14), channel_id=1, replica_groups=mesh['bin'=8,'col'=16] {'bin'}, dimensions={0}, use_global_device_ids=true | all-gather | bytes 488448 | tf_op jit(solution)/shard_map/all_gather | solution.py:11
  184.1 0.4 while.77
  184.5 0.1 multiply_add_fusion
  184.6 0.1 broadcast.45
  184.7 1.0 while.78
  185.7 13.0 %all_gather.18 = f32[8,106,128]{2,1,0:T(8,128)S(1)} all-gather(f32[1,106,128]{2,1,0:T(8,128)S(1)} %slice.16), channel_id=1, replica_groups=mesh['bin'=8,'col'=16] {'bin'}, dimensions={0}, use_global_device_ids=true | all-gather | bytes 488448 | tf_op jit(solution)/shard_map/all_gather | solution.py:11
  198.8 0.5 while.79
  199.3 0.0 copy-done
  199.3 2.2 convolution_bitcast_fusion.1
  201.5 0.0 all-gather.4.cloned.1.call-update
  201.5 0.0 all-reduce.2.cloned.1.call-start
  201.6 107.4 %all-gather.4.cloned.1.call-done = f32[16,106,2048]{2,1,0:T(8,128)} async-done(((f32[16,106,128]{2,1,0:T(8,128)}), f32[16,106,2048]{2,1,0:T(8,128)}) %all-gather.4.cloned.1.call-update) | async-done | bytes 13893648 | tf_op jit(solution)/shard_map/all_gather | solution.py:112
  309.0 0.0 copy-done.5
  309.0 0.0 copy-start.1
  309.0 28.9 %multiply_reduce_fusion = f32[1024,106]{0,1:T(8,128)} fusion(f32[1024,16]{0,1:T(8,128)S(1)} %bitcast.91, f32[16,106,2048]{2,1,0:T(8,128)} %all-gather.4.cloned.1.call-done, s32[1024]{0:T(1024)S(1)} %add.147), kind=kOutput, calls=%fused_computation.30 | convolution fusion | flops 42686701568 | bytes 14397440 | tf_op jit(solution)/shard_map/dot_general | solution.py:94
  337.9 0.0 all-reduce.2.cloned.1.call-update
  338.0 0.0 copy-done.1
  338.0 1.2 copy.19
  339.1 57.6 %all-reduce.2.cloned.1.call-done = f32[106,1024]{1,0:T(8,128)} async-done(((f32[106,1024]{1,0:T(8,128)}), f32[106,1024]{1,0:T(8,128)}) %all-reduce.2.cloned.1.call-update) | async-done | bytes 434192 | tf_op jit(solution)/shard_map/psum | solution.py:122
  396.7 1.8 copy.77
  (498 shorter events, 13.6 us)
Async XLA Ops:
  7.2 192.1 %copy-start = (f32[16,106,106]{2,0,1:T(8,128)S(1)}, f32[16,106,106]{2,0,1:T(8,128)}, u32[]{:S(2)}) copy-start(f32[16,106,106]{2,0,1:T(8,128)} %param.23) | copy-start | bytes 2157316
  7.2 160.1 %reduce-scatter.2.cloned.1.call-start = ((), (), s32[]{:S(2)}) async-start(), calls=%async_computation.1 | async-start | bytes 15597568 | tf_op jit(solution)/shard_map/reduce_scatter | solution.py:108
  17.9 6.6 %copy-start.3 = (s32[1024]{0:T(1024)S(1)}, s32[1024]{0:T(1024)}, u32[]{:S(2)}) copy-start(s32[1024]{0:T(1024)} %param.19) | copy-start | bytes 12292
  62.5 0.7 copy-start.4
  62.5 104.8 %copy-start.2 = (f32[16,106,128]{2,0,1:T(8,128)S(1)}, f32[16,106,128]{2,0,1:T(8,128)}, u32[]{:S(2)}) copy-start(f32[16,106,128]{2,0,1:T(8,128)} %param.21) | copy-start | bytes 2605060
  62.6 246.4 %all-gather.4.cloned.1.call-start = ((), (), s32[]{:S(2)}) async-start(), calls=%async_computation.2 | async-start | bytes 15597568 | tf_op jit(solution)/shard_map/all_gather | solution.py:112
  168.8 140.2 %copy-start.5 = (f32[16,1024]{1,0:T(8,128)S(1)}, f32[16,1024]{1,0:T(8,128)}, u32[]{:S(2)}) copy-start(f32[16,1024]{1,0:T(8,128)} %param.20) | copy-start | bytes 196612
  201.5 195.2 %all-reduce.2.cloned.1.call-start = ((), (), s32[]{:S(2)}) async-start(), calls=%async_computation.3 | async-start | bytes 917504 | tf_op jit(solution)/shard_map/psum | solution.py:122
  309.0 29.0 %copy-start.1 = (f32[16,106,128]{2,1,0:T(8,128)S(1)}, f32[16,106,128]{2,1,0:T(8,128)}, u32[]{:S(2)}) copy-start(f32[16,106,128]{2,1,0:T(8,128)} %convolution_bitcast_fusion.1) | copy-start | bytes 2605060
Sparse Core Ops, SparseCore 0:
  62.7 104.6 reduce-scatter.1
  201.7 107.2 all-gather.3
  338.1 58.6 all-reduce.1
where the time goes:
time: 407 us; the launch traced here: 405 us
  waiting for transfers between devices  234 us (57%)
  matrix products  58.7 us (14%)
  blocking collectives  47.4 us (12%)
  local copies, waits for them, and re-layouts  40.6 us (10%)
  between operations  14 us (3%)
  other arithmetic  6.03 us (1%)
    all_gather x1, waiting for transfers between devices, local(): portion = lax.all_gather(new_state, 'col', axis=2, tiled=True)  107 us
    reduce_scatter x1, waiting for transfers between devices, local(): lax.psum_scatter(col_terms, 'col', scatter_dimension=2, tiled=True)  69.3 us
    psum x1, waiting for transfers between devices, local(): les_species = lax.psum(partial_species, 'bin')  57.6 us
    all_gather x4, blocking collectives, prefix(): everything = jax.tree.map(lambda part: lax.all_gather(part, axis), array)  47.4 us
    dot_general x1, matrix products, contract_last(): lax.dot_general(left_mat, right_mat, (((1,), (1,)), ((), ())), precision=...  28.9 us
    dot_general x1, matrix products, local(): jnp.dot(flat_source, member, precision=highest)  27.6 us
    unnamed x17, local copies, waits for them, and re-layouts  13.5 us
    reshape x1, local copies, waits for them, and re-layouts, local(): jnp.dot(flat_source, member, precision=highest)  10.4 us
  transfers between devices with their start and end apart: 3, of which 3 were waited for; matrix products, arithmetic and copies ran while one was open for 3% of the time, Pallas kernels for 0%

commit v1 on v0

--- a/solution.py
+++ b/solution.py
@@ -1,9 +1,202 @@
 import jax
 import jax.numpy as jnp
 from jax import lax
+from jax.experimental import pallas as pl
+from jax.experimental.pallas import tpu as pltpu
 from jax.sharding import PartitionSpec as P
 
 highest = lax.Precision.HIGHEST
+SIDE = 4
+TOP = 56
+
+
+def split_bf16(value):
+    high = value.astype(jnp.bfloat16)
+    return high, (value - high.astype(jnp.float32)).astype(jnp.bfloat16)
+
+
+def scatter_kernel(
+    source, relative, prior, right, staged, lhs, onehot, part, relay1, got1, relay2, got2, load_sem, send_sem, recv_sem
+):
+    bins, species, cells = source.shape
+    half = bins // 2
+    pad = lhs.shape[0] // 4
+    wide = part.shape[-1]
+    col = lax.axis_index("col")
+    z, x = col // SIDE, lax.rem(col, SIDE)
+    x_up, x_down = z * SIDE + lax.rem(x + 1, SIDE), z * SIDE + lax.rem(x + SIDE - 1, SIDE)
+    z_up, z_down = lax.rem(z + 1, SIDE) * SIDE + x, lax.rem(z + SIDE - 1, SIDE) * SIDE + x
+
+    def load(step, slot):
+        return [
+            pltpu.make_async_copy(source.at[step + k * half], staged.at[slot, k], load_sem.at[slot, k]) for k in range(2)
+        ]
+
+    for copy in load(0, 0):
+        copy.start()
+    barrier = pltpu.get_barrier_semaphore()
+    for other in (x_up, x_down, z_up, z_down):
+        pl.semaphore_signal(barrier, inc=1, device_id={"col": other}, device_id_type=pl.DeviceIdType.MESH)
+
+    lhs[...] = jnp.zeros_like(lhs)
+    for n in range(SIDE):
+        span = SIDE * wide
+        ids = lax.broadcasted_iota(jnp.int32, (cells, span), 1) + n * span
+        onehot[:, n * span : (n + 1) * span] = (relative[...] == ids).astype(jnp.float32).astype(jnp.bfloat16)
+    pl.semaphore_wait(barrier, 4)
+
+    def copies(b, ways):
+        up1, down1, up2, down2 = ways
+        low, high = pl.ds(0, TOP), pl.ds(TOP, species - TOP)
+        table = [
+            (part.at[b, 2, pl.ds(0, 2)], relay1.at[b, 0], up1),
+            (part.at[b, 2, pl.ds(2, 2)], relay1.at[b, 1], down1),
+            (part.at[b, 1, pl.ds(2, 2)], got1.at[b, 0, pl.ds(2, 2)], up1),
+            (part.at[b, 3, pl.ds(0, 2)], got1.at[b, 1, pl.ds(0, 2)], down1),
+            (part.at[b, 1, pl.ds(0, 2)], got1.at[b, 0, pl.ds(0, 2)], up1),
+            (part.at[b, 3, pl.ds(2, 2)], got1.at[b, 1, pl.ds(2, 2)], down1),
+            (part.at[b, 0, 2, low], relay2.at[b, 0], up2),
+            (part.at[b, 0, 2, high], relay2.at[b, 1, pl.ds(0, species - TOP)], down2),
+            (part.at[b, 0, 1, high], got2.at[b, 0, high], up2),
+            (part.at[b, 0, 3, low], got2.at[b, 1, low], down2),
+            (part.at[b, 0, 1, low], got2.at[b, 0, low], up2),
+            (part.at[b, 0, 3, high], got2.at[b, 1, high], down2),
+        ]
+
+        def make(k):
+            src, dst, who = table[k]
+            return pltpu.make_async_remote_copy(
+                src_ref=src,
+                dst_ref=dst,
+                send_sem=send_sem.at[b, k],
+                recv_sem=recv_sem.at[b, k],
+                device_id={"col": who},
+                device_id_type=pl.DeviceIdType.MESH,
+            )
+
+        return make
+
+    ways_of = ((x_up, x_down, z_up, z_down), (z_up, z_down, x_up, x_down))
+
+    def both(step):
+        return [copies(step + k * half, ways_of[k]) for k in range(2)]
+
+    def turn(t, carry):
+        @pl.when(t < half)
+        def produce():
+            slot = lax.rem(t, 2)
+            for copy in load(t, slot):
+                copy.wait()
+
+            @pl.when(t + 1 < half)
+            def ahead():
+                for copy in load(t + 1, 1 - slot):
+                    copy.start()
+
+            for k in range(2):
+                high, low = split_bf16(staged[slot, k])
+                lhs[k * pad : k * pad + species, :] = high
+                lhs[(2 + k) * pad : (2 + k) * pad + species, :] = low
+            sends = both(t)
+            for dx in (2, 1, 3, 0):
+                span = SIDE * wide
+                out = jnp.dot(
+                    lhs[...], onehot[:, dx * span : (dx + 1) * span], preferred_element_type=jnp.float32
+                )
+                for k in range(2):
+                    total = out[k * pad : k * pad + species] + out[(2 + k) * pad : (2 + k) * pad + species]
+                    for dz in range(SIDE):
+                        piece = total[:, dz * wide : (dz + 1) * wide]
+                        if k == 0:
+                            part[t, dx, dz] = piece
+                        else:
+                            part[t + half, dz, dx] = piece
+                if dx == 2:
+                    for m in (0, 1):
+                        sends[0](m).start()
+                if dx == 1:
+                    sends[0](2).start()
+                if dx == 3:
+                    sends[0](3).start()
+            for m in range(4):
+                sends[1](m).start()
+
+        @pl.when((t >= 1) & (t < half + 1))
+        def forward_first():
+            for k, flight in enumerate(both(t - 1)):
+                b = t - 1 + k * half
+                flight(0).wait_recv()
+                part[b, 1, 0:2] = part[b, 1, 0:2] + relay1[b, 0]
+                flight(4).start()
+                flight(1).wait_recv()
+                part[b, 3, 2:4] = part[b, 3, 2:4] + relay1[b, 1]
+                flight(5).start()
+
+        @pl.when((t >= 2) & (t < half + 2))
+        def second_stage():
+            for k, flight in enumerate(both(t - 2)):
+                b = t - 2 + k * half
+                for m in (2, 3, 4, 5):
+                    flight(m).wait_recv()
+                part[b, 0] = part[b, 0] + got1[b, 0] + got1[b, 1]
+                for m in (6, 7, 8, 9):
+                    flight(m).start()
+
+        @pl.when((t >= 3) & (t < half + 3))
+        def forward_second():
+            for k, flight in enumerate(both(t - 3)):
+                b = t - 3 + k * half
+                flight(6).wait_recv()
+                part[b, 0, 1, 0:TOP] = part[b, 0, 1, 0:TOP] + relay2[b, 0]
+                flight(10).start()
+                flight(7).wait_recv()
+                part[b, 0, 3, TOP:species] = part[b, 0, 3, TOP:species] + relay2[b, 1, 0 : species - TOP]
+                flight(11).start()
+
+        @pl.when(t >= 4)
+        def finish():
+            for k, flight in enumerate(both(t - 4)):
+                b = t - 4 + k * half
+                for m in (8, 9, 10, 11):
+                    flight(m).wait_recv()
+                right[b] = prior[b] + (part[b, 0, 0] + got2[b, 0] + got2[b, 1])
+                for m in range(12):
+                    flight(m).wait_send()
+
+        return carry
+
+    lax.fori_loop(0, half + 4, turn, 0)
+
+
+def scatter_and_reduce(les_source, relative, prior):
+    bins, species, cells = les_source.shape
+    wide = prior.shape[2]
+    pad = -(-species // 16) * 16
+    return pl.pallas_call(
+        scatter_kernel,
+        out_shape=jax.ShapeDtypeStruct(prior.shape, jnp.float32),
+        in_specs=[
+            pl.BlockSpec(memory_space=pl.ANY),
+            pl.BlockSpec(memory_space=pltpu.VMEM),
+            pl.BlockSpec(memory_space=pltpu.VMEM),
+        ],
+        out_specs=pl.BlockSpec(memory_space=pltpu.VMEM),
+        scratch_shapes=[
+            pltpu.VMEM((2, 2, species, cells), jnp.float32),
+            pltpu.VMEM((4 * pad, cells), jnp.bfloat16),
+            pltpu.VMEM((cells, SIDE * SIDE * wide), jnp.bfloat16),
+            pltpu.VMEM((bins, SIDE, SIDE, species, wide), jnp.float32),
+            pltpu.VMEM((bins, 2, 2, species, wide), jnp.float32),
+            pltpu.VMEM((bins, 2, SIDE, species, wide), jnp.float32),
+            pltpu.VMEM((bins, 2, TOP, wide), jnp.float32),
+            pltpu.VMEM((bins, 2, species, wide), jnp.float32),
+            pltpu.SemaphoreType.DMA((2, 2)),
+            pltpu.SemaphoreType.DMA((bins, 12)),
+            pltpu.SemaphoreType.DMA((bins, 12)),
+        ],
+        compiler_params=pltpu.CompilerParams(collective_id=0, has_side_effects=True, vmem_limit_bytes=58 << 20),
+        name="scatter_and_reduce",
+    )(les_source, relative, prior)
 
 
 def prefix(array, axis, combine, identity, reverse):
@@ -44,6 +237,14 @@
         advance, jnp.zeros(coeffs.shape[1:], jnp.float32), coeffs
     )
     return (ratio_values, pivot_values)
+
+
+def running_product(rows, reverse):
+    def multiply(before, row):
+        new = before * row
+        return new, new
+
+    return lax.scan(multiply, jnp.ones(rows.shape[1:], jnp.float32), rows, reverse=reverse)[1]
 
 
 def bin_solve(right_hand_side, dissip):
@@ -65,7 +266,7 @@
     unused_item, partial_elimination = lax.scan(
         eliminate_step, zeroed_plane, (ratio_values, pivot_values, right_hand_side)
     )
-    growth_factor = jnp.cumprod(ratio_values, axis=0)
+    growth_factor = running_product(ratio_values, False)
     unused_item, incoming_entry = prefix(
         (growth_factor[-1], partial_elimination[-1]),
         "bin",
@@ -83,7 +284,7 @@
     unused_item, partial_back = lax.scan(
         substitute, zeroed_plane, (ratio_values, eliminated_rows), reverse=True
     )
-    decay_back = jnp.cumprod(ratio_values[::-1], axis=0)[::-1]
+    decay_back = running_product(ratio_values, True)
     unused_item, outgoing = prefix(
         (decay_back[0], partial_back[0]), "bin", compose_affine, (identity_line, zeroed_plane), True
     )
@@ -97,16 +298,13 @@
 def local(les_source, cell_owner, cell_slot, pdf_weight, prior_state, dissip, react_inverse):
     local_bins, species, cell_num = les_source.shape
     col_local = prior_state.shape[2]
-    groups = lax.axis_size("col")
-    flat_source = les_source.reshape(local_bins * species, cell_num)
-    column = cell_owner[:, 0] * col_local + cell_slot
-    all_cols = col_local * groups
-    member = (column[:, None] == jnp.arange(all_cols, dtype=jnp.int32)[None, :]).astype(jnp.float32)
-    col_terms = jnp.dot(flat_source, member, precision=highest).reshape(
-        local_bins, species, all_cols
-    )
-    cond_source = lax.psum_scatter(col_terms, "col", scatter_dimension=2, tiled=True)
-    right_hand_side = prior_state + cond_source
+    owner = cell_owner[:, 0]
+    column = owner * col_local + cell_slot
+    me = lax.axis_index("col")
+    ahead_z = (owner // SIDE - me // SIDE) % SIDE
+    ahead_x = (owner % SIDE - me % SIDE) % SIDE
+    relative = ((ahead_x * SIDE + ahead_z) * col_local + cell_slot)[:, None]
+    right_hand_side = scatter_and_reduce(les_source, relative, prior_state)
     solved_values = bin_solve(right_hand_side, dissip)
     new_state = jnp.einsum("ist,itc->isc", react_inverse, solved_values, precision=highest)
     portion = lax.all_gather(new_state, "col", axis=2, tiled=True)

time: 407 us -> 384 us (0.943)
  Pallas kernels: 0 us -> 85.3 us
  waiting for transfers between devices: 234 us -> 165 us
  matrix products: 58.7 us -> 31.1 us
  local copies, waits for them, and re-layouts: 40.6 us -> 27.8 us
    pallas_call x0 -> x1, Pallas kernels: none -> 85.3 us  [scatter_and_reduce(): pl.pallas_call(scatter_kernel, out_shape=jax.ShapeDtypeStruct(prior.shape...]
    reduce_scatter x1 -> x0, waiting for transfers between devices: 69.3 us -> none  [local(): lax.psum_scatter(col_terms, 'col', scatter_dimension=2, tiled=True)]
    dot_general x1 -> x0, matrix products: 27.6 us -> none  [local(): jnp.dot(flat_source, member, precision=highest)]
    reshape x2 -> x0, local copies, waits for them, and re-layouts: 17 us -> none  [the longest x1 10.4 us: local(): jnp.dot(flat_source, member, precision=highest)]
    unnamed x17 -> x12, local copies, waits for them, and re-layouts: 13.5 us -> 15.4 us
  transfers between devices with their start and end apart: 3 -> 2, of which waited for: 3 -> 2; matrix products, arithmetic and copies ran while one was open for 3% -> 0% of each run, Pallas kernels for 0% -> 0%
where the time goes in v1:
time: 384 us; the launch traced here: 382 us
  waiting for transfers between devices  165 us (43%)
  Pallas kernels  85.3 us (22%)
  blocking collectives  48.2 us (13%)
  matrix products  31.1 us (8%)
  local copies, waits for them, and re-layouts  27.8 us (7%)
  between operations  14.3 us (4%)
  other arithmetic  5.87 us (2%)
  loops' own time  4.35 us (1%)
    all_gather x1, waiting for transfers between devices, local(): portion = lax.all_gather(new_state, 'col', axis=2, tiled=True)  107 us
    pallas_call x1, Pallas kernels, scatter_and_reduce(): pl.pallas_call(scatter_kernel, out_shape=jax.ShapeDtypeStruct(prior.shape...  85.3 us
    psum x1, waiting for transfers between devices, local(): les_species = lax.psum(partial_species, 'bin')  57.6 us
    all_gather x4, blocking collectives, prefix(): everything = jax.tree.map(lambda part: lax.all_gather(part, axis), array)  48.2 us
    dot_general x1, matrix products, contract_last(): lax.dot_general(left_mat, right_mat, (((1,), (1,)), ((), ())), precision=...  28.9 us
    unnamed x12, local copies, waits for them, and re-layouts  15.4 us
    dynamic_update_slice x256, local copies, waits for them, and re-layouts, pivot_chain(): lax.scan(advance, jnp.zeros(coeffs.shape[1:], jnp.float32), coeffs)  9.5 us
  transfers between devices with their start and end apart: 2, of which 2 were waited for; matrix products, arithmetic and copies ran while one was open for 0% of the time, Pallas kernels for 0%

profile of v1, /device:TPU:1, one launch (start us, length us, event | category | flops | bytes accessed | tf_op | source)
XLA Modules:
  0.0 382.0 jit_solution(10186932604527607661)
XLA Ops:
  7.2 0.0 copy-start
  7.2 0.0 all-gather.4.cloned.1.call-start
  7.3 0.8 broadcast_multiply_fusion
  8.2 14.4 %while.105 = (s32[]{:T(128)}, f32[128]{0:T(128)S(1)}, f32[128,128]{1,0:T(8,128)S(1)}, f32[128,128]{1,0:T(8,128)S(1)}, f32[128,128]{1,0:T(8,128)S(1)}, /*index=5*/s32[]{:T(128)}, s32[]{:T(128)}) while((s32[]{:T(128)}, f32[128]{0:T(128)S(1)}, f32[128,128]{1,0:T(8,128)S(1)}, f32[128,128]{1,0:T(8,128)S(1)}, f32[128,128]{1,0:T(8,128)S(1)}, ...), condition=%wide.region_1.2_spmd.clone, body=%wide.region_0.1_spmd.clone.sunk | while | flops 771 | bytes 4203 | solution.py:236
  22.6 1.1 while.103
  23.8 1.2 while.104
  25.0 12.1 %all-gather = f32[8,1,128]{2,1,0:T(1,128)S(1)} all-gather(f32[1,1,128]{2,1,0:T(1,128)S(1)} %slice_bitcast_fusion.1), channel_id=1, replica_groups=mesh['bin'=8,'col'=16] {'bin'}, dimensions={0}, use_global_device_ids=true | all-gather | bytes 4608 | tf_op jit(solution)/shard_map/all_gather | solution.py:204
  37.0 8.0 %all-gather.1 = f32[8,1,128]{2,1,0:T(1,128)S(1)} all-gather(f32[1,1,128]{2,1,0:T(1,128)S(1)} %slice_bitcast_fusion), channel_id=1, replica_groups=mesh['bin'=8,'col'=16] {'bin'}, dimensions={0}, use_global_device_ids=true | all-gather | bytes 4608 | tf_op jit(solution)/shard_map/all_gather | solution.py:204
  45.1 0.7 multiply_add_fusion.1
  45.8 1.0 copy.19.relative
  46.8 2.4 copy.20.prior
  49.2 10.0 %copy.18.source = f32[16,106,1024]{2,1,0:T(8,128)} copy(f32[16,106,1024]{2,0,1:T(8,128)} %param.21) | data formatting | bytes 13893632 | tf_op args[0]
  59.2 85.3 %scatter_and_reduce.1 = f32[16,106,128]{2,1,0:T(8,128)S(1)} custom-call(f32[16,106,1024]{2,1,0:T(8,128)} %copy.18.source, s32[1024,1]{1,0:T(8,128)} %copy.19.relative, f32[16,106,128]{2,1,0:T(8,128)} %copy.20.prior), custom_call_target="tpu_custom_call" | custom-call | tf_op jit(solution)/shard_map/scatter_and_reduce/pallas_call | solution.py:175
  144.5 0.0 copy-start.2
  144.5 0.1 broadcast.68.clone
  144.6 1.0 while.106
  145.7 15.1 %all_gather.16 = f32[8,106,128]{2,1,0:T(8,128)S(1)} all-gather(f32[1,106,128]{2,1,0:T(8,128)S(1)} %slice.13), channel_id=1, replica_groups=mesh['bin'=8,'col'=16] {'bin'}, dimensions={0}, use_global_device_ids=true | all-gather | bytes 488448 | tf_op jit(solution)/shard_map/all_gather | solution.py:204
  160.8 0.5 while.107
  161.2 0.1 multiply_add_fusion
  161.3 0.1 broadcast.68
  161.4 1.1 while.108
  162.5 13.0 %all_gather.18 = f32[8,106,128]{2,1,0:T(8,128)S(1)} all-gather(f32[1,106,128]{2,1,0:T(8,128)S(1)} %slice.15), channel_id=1, replica_groups=mesh['bin'=8,'col'=16] {'bin'}, dimensions={0}, use_global_device_ids=true | all-gather | bytes 488448 | tf_op jit(solution)/shard_map/all_gather | solution.py:204
  175.5 0.5 while.109
  176.0 0.0 copy-done
  176.0 2.2 convolution_bitcast_fusion
  178.3 0.0 all-gather.4.cloned.1.call-update
  178.3 0.2 all-reduce.2.cloned.1.call-start
  178.5 107.0 %all-gather.4.cloned.1.call-done = f32[16,106,2048]{2,1,0:T(8,128)} async-done(((f32[16,106,128]{2,1,0:T(8,128)}), f32[16,106,2048]{2,1,0:T(8,128)}) %all-gather.4.cloned.1.call-update) | async-done | bytes 13893648 | tf_op jit(solution)/shard_map/all_gather | solution.py:310
  285.5 0.0 copy-done.2
  285.5 0.0 copy-start.1
  285.5 28.9 %multiply_reduce_fusion = f32[1024,106]{0,1:T(8,128)} fusion(f32[1024,16]{0,1:T(8,128)S(1)} %bitcast.106, f32[16,106,2048]{2,1,0:T(8,128)} %all-gather.4.cloned.1.call-done, s32[1024]{0:T(1024)S(1)} %get-tuple-element.680), kind=kOutput, calls=%fused_computation.31 | convolution fusion | flops 42686701568 | bytes 14397440 | tf_op jit(solution)/shard_map/dot_general | solution.py:295
  314.5 0.0 all-reduce.2.cloned.1.call-update
  314.5 0.0 copy-done.1
  314.5 1.2 copy.22
  315.7 57.6 %all-reduce.2.cloned.1.call-done = f32[106,1024]{1,0:T(8,128)} async-done(((f32[106,1024]{1,0:T(8,128)}), f32[106,1024]{1,0:T(8,128)}) %all-reduce.2.cloned.1.call-update) | async-done | bytes 434192 | tf_op jit(solution)/shard_map/psum | solution.py:320
  373.3 1.8 copy.99
  (561 shorter events, 15.5 us)
Async XLA Ops:
  7.2 168.9 %copy-start = (f32[16,106,106]{2,0,1:T(8,128)S(1)}, f32[16,106,106]{2,0,1:T(8,128)}, u32[]{:S(2)}) copy-start(f32[16,106,106]{2,0,1:T(8,128)} %param.27) | copy-start | bytes 2157316
  7.2 278.3 %all-gather.4.cloned.1.call-start = ((), (), s32[]{:S(2)}) async-start(), calls=%async_computation | async-start | bytes 15597568 | tf_op jit(solution)/shard_map/all_gather | solution.py:310
  144.5 141.0 %copy-start.2 = (f32[16,1024]{1,0:T(8,128)S(1)}, f32[16,1024]{1,0:T(8,128)}, u32[]{:S(2)}) copy-start(f32[16,1024]{1,0:T(8,128)} %param.24) | copy-start | bytes 196612
  178.3 195.0 %all-reduce.2.cloned.1.call-start = ((), (), s32[]{:S(2)}) async-start(), calls=%async_computation.1 | async-start | bytes 917504 | tf_op jit(solution)/shard_map/psum | solution.py:320
  285.5 29.0 %copy-start.1 = (f32[16,106,128]{2,1,0:T(8,128)S(1)}, f32[16,106,128]{2,1,0:T(8,128)}, u32[]{:S(2)}) copy-start(f32[16,106,128]{2,1,0:T(8,128)} %convolution_bitcast_fusion) | copy-start | bytes 2605060
Sparse Core Ops, SparseCore 0:
  178.4 107.0 all-gather.3
  314.6 58.6 all-reduce.1

commit v2 on v0

v2 whole, which is shorter than its diff:
```python
import jax
import jax.numpy as jnp
from jax import lax
from jax.experimental import pallas as pl
from jax.experimental.pallas import tpu as pltpu
from jax.sharding import PartitionSpec as P

SIDE = 4
OWNERS = SIDE * SIDE
ROWS = 112
STEPS = 7
MESH = pl.DeviceIdType.MESH


def split_bf16(value):
    high = value.astype(jnp.bfloat16)
    return high, (value - high.astype(jnp.float32)).astype(jnp.bfloat16)


def bf16_where(mask):
    return mask.astype(jnp.float32).astype(jnp.bfloat16)


def step_kernel(
    source, owner, slot, pdf, prior, dissip, react,
    state, les,
    staged, lhs, onehot, packing, before, part, relay1, got1, relay2, got2,
    prior_v, react_v, wide_react, react3, right, ratio, inverse, grown, carried, decayed,
    packed, got_packed, picks, lines, edges, got_edges, ends, got_ends, solved, picked,
    sums, from_twin, relay_b, got_b, total, back, unpacked, gathered,
    load_sem, send_sem, recv_sem, pack_send, pack_recv, edge_send, edge_recv, end_send, end_recv,
    bin_send, bin_recv, back_send, back_recv, all_send, all_recv,
):
    cells = source.shape[1]
    cols = prior.shape[1]
    bins = pdf.shape[0]
    species = prior.shape[0] // bins
    half = prior.shape[0] // 2
    last = half - STEPS * ROWS
    span = SIDE * cols
    padded = solved.shape[1]
    col, bin_ = lax.axis_index("col"), lax.axis_index("bin")
    z, x = col // SIDE, lax.rem(col, SIDE)
    y, core = bin_ // 2, lax.rem(bin_, 2)
    groups = 2 * SIDE

    def col_at(dz, dx):
        return lax.rem(z + dz + SIDE, SIDE) * SIDE + lax.rem(x + dx + SIDE, SIDE)

    def bin_at(dy, other=False):
        return lax.rem(y + dy + SIDE, SIDE) * 2 + (1 - core if other else core)

    x_up, x_down, z_up, z_down = col_at(0, 1), col_at(0, -1), col_at(1, 0), col_at(-1, 0)
    twin = bin_at(0, True)

    def remote(src, dst, sends, recvs, at, axis, who):
        return pltpu.make_async_remote_copy(
            src_ref=src, dst_ref=dst, send_sem=sends.at[at], recv_sem=recvs.at[at],
            device_id={axis: who}, device_id_type=MESH,
        )

    def first_row(c, k):
        return pl.multiple_of(c * ROWS + k * half, 8)

    def load(c, rows, where, k):
        return pltpu.make_async_copy(
            source.at[pl.ds(first_row(c, k), rows)], staged.at[where, k, pl.ds(0, rows)], load_sem.at[where, k]
        )

    def prior_copy():
        return pltpu.make_async_copy(prior, prior_v, load_sem.at[2, 0])

    def react_copy():
        return pltpu.make_async_copy(react, react_v, load_sem.at[2, 1])

    for k in range(2):
        load(0, ROWS, 0, k).start()
    react_copy().start()
    prior_copy().start()
    barrier = pltpu.get_barrier_semaphore()
    for dx in range(SIDE):
        for dz in range(SIDE):
            if dx or dz:
                pl.semaphore_signal(barrier, inc=1, device_id={"col": col_at(dz, dx)}, device_id_type=MESH)
    for d in range(1, groups):
        pl.semaphore_signal(barrier, inc=1, device_id={"bin": lax.rem(bin_ + d, groups)}, device_id_type=MESH)

    ahead = ((owner[...] & (SIDE - 1)) - x) & (SIDE - 1)
    block = ahead * SIDE + (((owner[...] >> 2) - z) & (SIDE - 1))

    def expand(index, target):
        lane = lax.broadcasted_iota(jnp.int32, (128, 128), 1).astype(jnp.float32)
        for q in range(cells // 128):
            tall = jnp.transpose(jnp.broadcast_to(index[:, q * 128 : (q + 1) * 128], (128, 128)))
            for n in range(target.shape[1] // 128):
                target[q * 128 : (q + 1) * 128, n * 128 : (n + 1) * 128] = bf16_where(tall == lane + float(n * 128))

    expand((block * cols + slot[...]).astype(jnp.float32), onehot)
    pl.semaphore_wait(barrier, OWNERS - 1 + groups - 1)

    ways_of = ((x_up, x_down, z_up, z_down), (z_up, z_down, x_up, x_down))

    def flight(c, rows, k):
        b = c + k * (STEPS + 1)
        up1, down1, up2, down2 = ways_of[k]
        every, low, high = pl.ds(0, rows), pl.ds(0, rows // 2), pl.ds(rows // 2, rows // 2)
        first, rest = pl.ds(0, 2), pl.ds(2, 2)
        table = [
            (part.at[b, 2, first, every], relay1.at[b, 0, :, every], up1),
            (part.at[b, 2, rest, every], relay1.at[b, 1, :, every], down1),
            (part.at[b, 1, rest, every], got1.at[b, 0, rest, every], up1),
            (part.at[b, 3, first, every], got1.at[b, 1, first, every], down1),
            (part.at[b, 1, first, every], got1.at[b, 0, first, every], up1),
            (part.at[b, 3, rest, every], got1.at[b, 1, rest, every], down1),
            (part.at[b, 0, 2, low], relay2.at[b, 0, low], up2),
            (part.at[b, 0, 2, high], relay2.at[b, 1, low], down2),
            (part.at[b, 0, 1, high], got2.at[b, 0, high], up2),
            (part.at[b, 0, 3, low], got2.at[b, 1, low], down2),
            (part.at[b, 0, 1, low], got2.at[b, 0, low], up2),
            (part.at[b, 0, 3, high], got2.at[b, 1, high], down2),
        ]

        def make(m):
            src, dst, who = table[m]
            return remote(src, dst, send_sem, recv_sem, (b, m), "col", who)

        return b, make

    def produce(c, rows):
        where = c % 2 if isinstance(c, int) else lax.rem(c, 2)
        for k in range(2):
            load(c, rows, where, k).wait()
        if not isinstance(c, int):

            @pl.when(c + 1 < STEPS)
            def full():
                for k in range(2):
                    load(c + 1, ROWS, 1 - where, k).start()

            @pl.when(c + 1 == STEPS)
            def short():
                for k in range(2):
                    load(STEPS, last, 1 - where, k).start()

        for k in range(2):
            high, low = split_bf16(staged[where, k, 0:rows])
            lhs[k * rows : (k + 1) * rows] = high
            lhs[(2 + k) * rows : (3 + k) * rows] = low
        trips = [flight(c, rows, k) for k in range(2)]
        for dx in (2, 1, 3, 0):
            out = jnp.dot(
                lhs[0 : 4 * rows], onehot[:, dx * span : (dx + 1) * span], preferred_element_type=jnp.float32
            )
            for k in range(2):
                both = out[k * rows : (k + 1) * rows] + out[(2 + k) * rows : (3 + k) * rows]
                for dz in range(SIDE):
                    piece = both[:, dz * cols : (dz + 1) * cols]
                    if k == 0:
                        part[trips[0][0], dx, dz, 0:rows] = piece
                    else:
                        part[trips[1][0], dz, dx, 0:rows] = piece
            for m in {2: (0, 1), 1: (2,), 3: (3,), 0: ()}[dx]:
                trips[0][1](m).start()
        for m in range(4):
            trips[1][1](m).start()

    def forward_first(c, rows):
        for k in range(2):
            b, make = flight(c, rows, k)
            make(0).wait_recv()
            part[b, 1, 0:2, 0:rows] = part[b, 1, 0:2, 0:rows] + relay1[b, 0, :, 0:rows]
            make(4).start()
            make(1).wait_recv()
            part[b, 3, 2:4, 0:rows] = part[b, 3, 2:4, 0:rows] + relay1[b, 1, :, 0:rows]
            make(5).start()

    def second_stage(c, rows):
        for k in range(2):
            b, make = flight(c, rows, k)
            for m in (2, 3, 4, 5):
                make(m).wait_recv()
            part[b, 0, :, 0:rows] = part[b, 0, :, 0:rows] + got1[b, 0, :, 0:rows] + got1[b, 1, :, 0:rows]
            for m in (6, 7, 8, 9):
                make(m).start()

    def forward_second(c, rows):
        low = rows // 2
        for k in range(2):
            b, make = flight(c, rows, k)
            make(6).wait_recv()
            part[b, 0, 1, 0:low] = part[b, 0, 1, 0:low] + relay2[b, 0, 0:low]
            make(10).start()
            make(7).wait_recv()
            part[b, 0, 3, low:rows] = part[b, 0, 3, low:rows] + relay2[b, 1, 0:low]
            make(11).start()

    def finish(c, rows):
        for k in range(2):
            b, make = flight(c, rows, k)
            for m in (8, 9, 10, 11):
                make(m).wait_recv()
            at = pl.ds(first_row(c, k), rows)
            right[at] = prior_v[at] + (part[b, 0, 0, 0:rows] + got2[b, 0, 0:rows] + got2[b, 1, 0:rows])
            for m in range(12):
                make(m).wait_send()

    def pack_copy(n):
        dx, dz = n // SIDE, n % SIDE
        return remote(packed.at[n], got_packed.at[n], pack_send, pack_recv, n, "col", col_at(dz, dx))

    def pack_weights():
        numbers = lax.broadcasted_iota(jnp.int32, (OWNERS, cells), 0)
        mine = numbers == owner[...]
        for q in range(cells // 128):
            rows_ = lax.broadcasted_iota(jnp.int32, (128, cells), 0) + q * 128
            before[q * 128 : (q + 1) * 128] = bf16_where(rows_ < lax.broadcasted_iota(jnp.int32, (128, cells), 1))
        counts = jnp.dot(bf16_where(mine), before[...], preferred_element_type=jnp.float32)
        rank = jnp.sum(jnp.where(mine, counts, 0.0), axis=0, keepdims=True)
        expand((block * 128).astype(jnp.float32) + rank, packing)
        high, low = split_bf16(pdf[...])
        slots = jnp.broadcast_to(slot[...].astype(jnp.float32), (bins, cells)).astype(jnp.bfloat16)
        for n in range(OWNERS):
            at = slice(n * 128, (n + 1) * 128)
            out = jnp.dot(
                jnp.concatenate([high, low, slots], axis=0), packing[:, at], preferred_element_type=jnp.float32
            )
            packed[n, 0:bins] = out[0:bins] + out[bins : 2 * bins]
            packed[n, bins : bins + 8] = out[2 * bins : 2 * bins + 8]
        for n in range(1, OWNERS):
            pack_copy(n).start()

    def take_weights():
        got_packed[0] = packed[0]
        for n in range(1, OWNERS):
            pack_copy(n).wait_recv()
        lane = lax.broadcasted_iota(jnp.int32, (cols, 128), 0).astype(jnp.float32)
        for n in range(OWNERS):
            hit = bf16_where(lane == got_packed[n, bins : bins + 1])
            at = slice(n % 2 * 128, (n % 2 + 1) * 128)
            picks[n // 2, 0:cols, at] = hit
            picks[n // 2, cols : 2 * cols, at] = hit

    def split_react():
        react_copy().wait()
        wide_react[...] = jnp.zeros_like(wide_react)
        wide_react[0 : species * bins, 0:species] = react_v[...]

        def one(i, carry):
            high, low = split_bf16(wide_react[pl.ds(i, ROWS, stride=bins)])
            react3[i, :, 0:128] = high
            react3[i, :, 128:256] = low
            react3[i, :, 256:384] = high
            return carry

        lax.fori_loop(0, bins, one, 0)
        solved[...] = jnp.zeros_like(solved)
        right[species * bins :] = jnp.zeros((right.shape[0] - species * bins, cols), jnp.float32)
        edges[groups - 1] = jnp.zeros_like(edges[groups - 1])
        sums[groups - 1] = jnp.zeros_like(sums[groups - 1])

    every_bin = bins * groups

    def pivots(low, high):
        strength = jnp.broadcast_to(dissip[...], (8, cols))

        def one(i, earlier):
            centre = (i.astype(jnp.float32) + 0.5) / every_bin
            diffusion = strength * (4.0 * centre * (1.0 - centre) + 0.05)
            pivot = 1.0 + 2.0 * diffusion - diffusion * earlier
            new = diffusion / pivot
            ratio[i] = new
            inverse[i] = 1.0 / pivot
            return new

        start = jnp.where(low == 0, jnp.zeros((8, cols), jnp.float32), ratio[jnp.maximum(low - 1, 0)])
        lax.fori_loop(low, high, one, start)

    def factors():
        def block_(m, carry):
            def grow(i, g):
                g = g * ratio[m * bins + i]
                grown[m * bins + i] = g
                return g

            lax.fori_loop(0, bins, grow, jnp.ones((8, cols), jnp.float32))

            def shrink(n, both):
                h, d = both
                i = m * bins + bins - 1 - n
                h = grown[i] + ratio[i] * h
                d = ratio[i] * d
                carried[i] = h
                decayed[i] = d
                return h, d

            lax.fori_loop(0, bins, shrink, (jnp.zeros((8, cols), jnp.float32), jnp.ones((8, cols), jnp.float32)))
            return carry

        lax.fori_loop(0, groups, block_, 0)

    def turn(t, carry):
        produce(t, ROWS)

        @pl.when(t >= 1)
        def _():
            forward_first(t - 1, ROWS)

        @pl.when(t == 1)
        def _():
            pack_weights()

        @pl.when(t == 0)
        def _():
            split_react()

        pivots(t * 20, jnp.minimum(t * 20 + 20, every_bin))

        @pl.when(t >= 2)
        def _():
            second_stage(t - 2, ROWS)

        @pl.when(t >= 3)
        def _():
            forward_second(t - 3, ROWS)

        @pl.when(t == 3)
        def _():
            prior_copy().wait()

        @pl.when(t >= 4)
        def _():
            finish(t - 4, ROWS)

        return carry

    lax.fori_loop(0, STEPS, turn, 0)
    stages = (produce, forward_first, second_stage, forward_second, finish)
    for t in range(STEPS, STEPS + len(stages)):
        for n, stage in enumerate(stages):
            if n <= t and t - n <= STEPS:
                stage(t - n, last if t - n == STEPS else ROWS)
        if t == STEPS:
            factors()
            take_weights()

    base = bin_ * bins
    value = jnp.zeros((ROWS, cols), jnp.float32)
    for i in range(bins):
        value = right[pl.ds(i, ROWS, stride=bins)] * inverse[base + i, 0:1] + ratio[base + i, 0:1] * value
        lines[i] = value
    for j in range(groups - 1):
        edges[j, 0] = value[16 * j : 16 * j + 16]
    value = jnp.zeros((ROWS, cols), jnp.float32)
    for i in reversed(range(bins)):
        value = lines[i] + ratio[base + i, 0:1] * value
        lines[i] = value
    for j in range(groups - 1):
        edges[j, 1] = value[16 * j : 16 * j + 16]

    def edge_copy(d):
        other = lax.rem(bin_ + d, groups)
        return remote(edges.at[other], got_edges.at[d], edge_send, edge_recv, d, "bin", other)

    for d in range(1, groups):
        edge_copy(d).start()
    got_edges[0] = edges[bin_]
    for d in range(1, groups):
        edge_copy(d).wait_recv()
    value = jnp.zeros((16, cols), jnp.float32)
    for m in range(groups):
        ends[m, 0] = value
        value = got_edges[lax.rem(bin_ - m + groups, groups), 0] + decayed[m * bins, 0:1] * value
    value = jnp.zeros((16, cols), jnp.float32)
    for m in reversed(range(groups)):
        ends[m, 1] = value
        value = (
            got_edges[lax.rem(bin_ - m + groups, groups), 1]
            + carried[m * bins, 0:1] * ends[m, 0]
            + decayed[m * bins, 0:1] * value
        )

    def end_copy(d):
        other = lax.rem(bin_ + d, groups)
        return remote(ends.at[other], got_ends.at[bin_], end_send, end_recv, d, "bin", other)

    def end_arrived(d):
        other = lax.rem(bin_ - d + groups, groups)
        return remote(ends.at[other], got_ends.at[other], end_send, end_recv, d, "bin", other)

    for d in range(1, groups):
        end_copy(d).start()
    got_ends[bin_] = ends[bin_]
    for d in range(1, groups):
        end_arrived(d).wait_recv()
    entering = jnp.concatenate([got_ends[j, 0] for j in range(groups - 1)], axis=0)
    leaving = jnp.concatenate([got_ends[j, 1] for j in range(groups - 1)], axis=0)

    for i in range(bins):
        value = lines[i] + carried[base + i, 0:1] * entering + decayed[base + i, 0:1] * leaving
        high, low = split_bf16(value)
        at = i % 2
        solved[at, 0:ROWS] = high
        solved[at, 128 : 128 + ROWS] = high
        solved[at, 256 : 256 + ROWS] = low
        new = jnp.dot(react3[i], solved[at], preferred_element_type=jnp.float32)
        state[pl.ds(i, species, stride=bins)] = new[0:species]
        high, low = split_bf16(new)
        picked[i * ROWS : (i + 1) * ROWS, 0:cols] = high
        picked[i * ROWS : (i + 1) * ROWS, cols : 2 * cols] = low

    def weigh(n, carry):
        out = jnp.dot(picked[...], picks[n], preferred_element_type=jnp.float32)
        for q in range(2):
            acc = jnp.zeros((ROWS, 128), jnp.float32)
            for i in range(bins):
                acc = acc + out[i * ROWS : (i + 1) * ROWS, q * 128 : (q + 1) * 128] * got_packed[2 * n + q, i : i + 1]
            for j in range(groups - 1):
                sums[j, 2 * n + q] = acc[16 * j : 16 * j + 16]
        return carry

    lax.fori_loop(0, OWNERS // 2, weigh, 0)

    def twin_copy(dy):
        return remote(sums.at[bin_at(dy, True)], from_twin.at[dy], bin_send, bin_recv, dy, "bin", twin)

    for dy in (2, 1, 3, 0):
        twin_copy(dy).start()
    y_up, y_down = bin_at(1), bin_at(-1)
    first, rest = pl.ds(0, OWNERS // 2), pl.ds(OWNERS // 2, OWNERS // 2)
    bin_table = [
        (sums.at[bin_at(2), first], relay_b.at[0], y_up),
        (sums.at[bin_at(2), rest], relay_b.at[1], y_down),
        (sums.at[bin_at(1), rest], got_b.at[0, rest], y_up),
        (sums.at[bin_at(3), first], got_b.at[1, first], y_down),
        (sums.at[bin_at(1), first], got_b.at[0, first], y_up),
        (sums.at[bin_at(3), rest], got_b.at[1, rest], y_down),
    ]

    def bin_copy(m):
        src, dst, who = bin_table[m]
        return remote(src, dst, bin_send, bin_recv, SIDE + m, "bin", who)

    for dy, then in ((2, (0, 1)), (1, (2,)), (3, (3,)), (0, ())):
        twin_copy(dy).wait_recv()
        j = bin_at(dy)
        sums[j] = sums[j] + from_twin[dy]
        for m in then:
            bin_copy(m).start()
    middle = OWNERS // 2
    bin_copy(0).wait_recv()
    sums[bin_at(1), 0:middle] = sums[bin_at(1), 0:middle] + relay_b[0]
    bin_copy(4).start()
    bin_copy(1).wait_recv()
    sums[bin_at(3), middle:OWNERS] = sums[bin_at(3), middle:OWNERS] + relay_b[1]
    bin_copy(5).start()
    for m in (2, 3, 4, 5):
        bin_copy(m).wait_recv()
    total[...] = sums[bin_] + got_b[0] + got_b[1]

    def back_copy(n):
        dx, dz = n // SIDE, n % SIDE
        return remote(total.at[n], back.at[n], back_send, back_recv, n, "col", col_at(-dz, -dx))

    for n in range(1, OWNERS):
        back_copy(n).start()
    back[0] = total[0]
    for n in range(OWNERS):
        if n:
            back_copy(n).wait_recv()
        high, low = split_bf16(back[n])
        unpacked[0:16, n * 128 : (n + 1) * 128] = high
        unpacked[16:32, n * 128 : (n + 1) * 128] = low
    out = lax.dot_general(
        unpacked[...], packing[...], (((1,), (1,)), ((), ())), preferred_element_type=jnp.float32
    )
    gathered[bin_] = out[0:16] + out[16:32]

    behind, ahead_, across = bin_at(-1), bin_at(1), bin_at(2)
    top, bottom = pl.ds(0, 8), pl.ds(8, 8)

    def all_copy(m):
        block_of, part_of, who = [
            (bin_, None, y_up),
            (bin_, None, y_down),
            (bin_, None, twin),
            (behind, top, y_up),
            (ahead_, bottom, y_down),
            (behind, None, twin),
            (ahead_, None, twin),
            (across, None, twin),
        ][m]
        ref = gathered.at[block_of] if part_of is None else gathered.at[block_of, part_of]
        return remote(ref, ref, all_send, all_recv, m, "bin", who)

    def all_arrived(m):
        block_of, part_of = [
            (behind, None),
            (ahead_, None),
            (twin, None),
            (across, top),
            (across, bottom),
            (bin_at(-1, True), None),
            (bin_at(1, True), None),
            (bin_at(2, True), None),
        ][m]
        ref = gathered.at[block_of] if part_of is None else gathered.at[block_of, part_of]
        return remote(ref, ref, all_send, all_recv, m, "bin", twin)

    for m in (0, 1, 2):
        all_copy(m).start()
    all_arrived(0).wait_recv()
    all_copy(3).start()
    all_copy(5).start()
    all_arrived(1).wait_recv()
    all_copy(4).start()
    all_copy(6).start()
    all_arrived(3).wait_recv()
    all_arrived(4).wait_recv()
    all_copy(7).start()
    for m in (2, 5, 6, 7):
        all_arrived(m).wait_recv()
    for j in range(groups):
        count = min(16, species - 16 * j)
        if count > 0:
            les[16 * j : 16 * j + count] = gathered[j, 0:count]

    for n in range(1, OWNERS):
        pack_copy(n).wait_send()
        back_copy(n).wait_send()
    for d in range(1, groups):
        edge_copy(d).wait_send()
        end_copy(d).wait_send()
    for dy in range(SIDE):
        twin_copy(dy).wait_send()
    for m in range(6):
        bin_copy(m).wait_send()
    for m in range(8):
        all_copy(m).wait_send()


def local(les_source, cell_owner, cell_slot, pdf_weight, prior_state, dissip, react_inverse):
    bins, species, cells = les_source.shape
    cols = prior_state.shape[2]
    groups = 2 * SIDE
    rows = bins * species
    chunks = 2 * (STEPS + 1)
    f32, bf16 = jnp.float32, jnp.bfloat16

    def by_species(array):
        return jnp.transpose(array, (1, 0, 2)).reshape(rows, array.shape[2])

    vmem, hbm, dma = pl.BlockSpec(memory_space=pltpu.VMEM), pl.BlockSpec(memory_space=pl.ANY), pltpu.SemaphoreType.DMA
    state, les = pl.pallas_call(
        step_kernel,
        out_shape=(jax.ShapeDtypeStruct((rows, cols), f32), jax.ShapeDtypeStruct((species, cells), f32)),
        in_specs=[hbm, vmem, vmem, vmem, hbm, vmem, hbm],
        out_specs=(vmem, vmem),
        scratch_shapes=[
            pltpu.VMEM((2, 2, ROWS, cells), f32),
            pltpu.VMEM((4 * ROWS, cells), bf16),
            pltpu.VMEM((cells, OWNERS * cols), bf16),
            pltpu.VMEM((cells, OWNERS * 128), bf16),
            pltpu.VMEM((cells, cells), bf16),
            pltpu.VMEM((chunks, SIDE, SIDE, ROWS, cols), f32),
            pltpu.VMEM((chunks, 2, 2, ROWS, cols), f32),
            pltpu.VMEM((chunks, 2, SIDE, ROWS, cols), f32),
            pltpu.VMEM((chunks, 2, ROWS // 2, cols), f32),
            pltpu.VMEM((chunks, 2, ROWS, cols), f32),
            pltpu.VMEM((rows, cols), f32),
            pltpu.VMEM((rows, species), f32),
            pltpu.VMEM((ROWS * bins, 128), f32),
            pltpu.VMEM((bins, ROWS, 384), bf16),
            pltpu.VMEM((ROWS * bins, cols), f32),
            pltpu.VMEM((bins * groups, 8, cols), f32),
            pltpu.VMEM((bins * groups, 8, cols), f32),
            pltpu.VMEM((bins * groups, 8, cols), f32),
            pltpu.VMEM((bins * groups, 8, cols), f32),
            pltpu.VMEM((bins * groups, 8, cols), f32),
            pltpu.VMEM((OWNERS, bins + 8, 128), f32),
            pltpu.VMEM((OWNERS, bins + 8, 128), f32),
            pltpu.VMEM((OWNERS // 2, 2 * cols, 256), bf16),
            pltpu.VMEM((bins, ROWS, cols), f32),
            pltpu.VMEM((groups, 2, 16, cols), f32),
            pltpu.VMEM((groups, 2, 16, cols), f32),
            pltpu.VMEM((groups, 2, 16, cols), f32),
            pltpu.VMEM((groups, 2, 16, cols), f32),
            pltpu.VMEM((2, 384, cols), bf16),
            pltpu.VMEM((bins * ROWS, 2 * cols), bf16),
            pltpu.VMEM((groups, OWNERS, 16, 128), f32),
            pltpu.VMEM((SIDE, OWNERS, 16, 128), f32),
            pltpu.VMEM((2, OWNERS // 2, 16, 128), f32),
            pltpu.VMEM((2, OWNERS, 16, 128), f32),
            pltpu.VMEM((OWNERS, 16, 128), f32),
            pltpu.VMEM((OWNERS, 16, 128), f32),
            pltpu.VMEM((32, OWNERS * 128), bf16),
            pltpu.VMEM((groups, 16, cells), f32),
            dma((3, 2)),
            dma((chunks, 12)),
            dma((chunks, 12)),
            dma((OWNERS,)),
            dma((OWNERS,)),
            dma((groups,)),
            dma((groups,)),
            dma((groups,)),
            dma((groups,)),
            dma((SIDE + 6,)),
            dma((SIDE + 6,)),
            dma((OWNERS,)),
            dma((OWNERS,)),
            dma((8,)),
            dma((8,)),
        ],
        compiler_params=pltpu.CompilerParams(collective_id=0, has_side_effects=True, vmem_limit_bytes=63 << 20),
        name="cmc_step",
    )(
        by_species(les_source),
        cell_owner.reshape(1, cells),
        cell_slot.reshape(1, cells),
        pdf_weight,
        by_species(prior_state),
        dissip.reshape(1, cols),
        by_species(react_inverse),
    )
    return jnp.transpose(state.reshape(species, bins, cols), (1, 0, 2)), les


def solution(mesh):
    placed = (
        P("bin", None, "col"),
        P("col", None),
        P("col"),
        P("bin", "col"),
        P("bin", None, "col"),
        P("col"),
        P("bin", None, None),
    )
    return jax.shard_map(
        local,
        mesh=mesh,
        in_specs=placed,
        out_specs=(P("bin", None, "col"), P(None, "col")),
        check_vma=False,
    )
```

time: 407 us -> 136 us (0.33)
  waiting for transfers between devices: 234 us -> 0 us
  Pallas kernels: 0 us -> 132 us
  matrix products: 58.7 us -> 0 us
  blocking collectives: 47.4 us -> 0 us
  local copies, waits for them, and re-layouts: 40.6 us -> 3.95 us
  between operations: 14 us -> 0.64 us
  other arithmetic: 6.03 us -> 0 us
    pallas_call x0 -> x1, Pallas kernels: none -> 132 us  [local(): pl.pallas_call(step_kernel, out_shape=(jax.ShapeDtypeStruct((rows, cols),...]
    all_gather x1 -> x0, waiting for transfers between devices: 107 us -> none  [local(): portion = lax.all_gather(new_state, 'col', axis=2, tiled=True)]
    reduce_scatter x1 -> x0, waiting for transfers between devices: 69.3 us -> none  [local(): lax.psum_scatter(col_terms, 'col', scatter_dimension=2, tiled=True)]
    dot_general x3 -> x0, matrix products: 58.7 us -> none  [the longest x1 28.9 us: contract_last(): lax.dot_general(left_mat, right_mat, (((1,), (1,)), ((), ())), precision=...]
    psum x1 -> x0, waiting for transfers between devices: 57.6 us -> none  [local(): les_species = lax.psum(partial_species, 'bin')]
    all_gather x4 -> x0, blocking collectives: 47.4 us -> none  [prefix(): everything = jax.tree.map(lambda part: lax.all_gather(part, axis), array)]
    reshape x2 -> x0, local copies, waits for them, and re-layouts: 17 us -> none  [the longest x1 10.4 us: local(): jnp.dot(flat_source, member, precision=highest)]
    unnamed x17 -> x2, local copies, waits for them, and re-layouts: 13.5 us -> 3.95 us
  transfers between devices with their start and end apart: 3 -> 0, of which waited for: 3 -> 0; matrix products, arithmetic and copies ran while one was open for 3% -> 0% of each run, Pallas kernels for 0% -> 0%
where the time goes in v2:
time: 136 us
  Pallas kernels  132 us (97%)
  local copies, waits for them, and re-layouts  3.95 us (3%)
    pallas_call x1, Pallas kernels, local(): pl.pallas_call(step_kernel, out_shape=(jax.ShapeDtypeStruct((rows, cols),...  132 us
    unnamed x2, local copies, waits for them, and re-layouts  3.95 us

profile of v2, /device:TPU:1, one launch (start us, length us, event | category | flops | bytes accessed | tf_op | source)
XLA Modules:
  0.0 136.1 jit_solution(11555584081855651092)
XLA Ops:
  0.6 131.5 %cmc_step.1 = (f32[1696,128]{1,0:T(8,128)}, f32[106,1024]{1,0:T(8,128)}) custom-call(f32[1696,1024]{1,0:T(8,128)} %bitcast.15, s32[1,1024]{1,0:T(1,128)} %bitcast.19, s32[1,1024]{1,0:T(1,128)} %bitcast.20, f32[16,1024]{1,0:T(8,128)} %pdf.1, f32[1696,128]{1,0:T(8,128)} %bitcast.16, f32[1,128]{1,0:T(1,128)} %bitcast.21, f32[1696,106]{1,0:T(8,128)} %bitcast.17), custom_call_target="tpu_custom_call" | custom-call | tf_op jit(solution)/shard_map/cmc_step/pallas_call | solution.py:553
  132.2 2.1 %copy.11 = f32[16,106,128]{2,0,1:T(8,128)} copy(f32[16,106,128]{2,0,1:T(8,128)} %bitcast.18) | data formatting | bytes 1736704
  134.3 1.8 %copy.12 = f32[106,1024]{1,0:T(8,128)} copy(f32[106,1024]{1,0:T(8,128)} %get-tuple-element.9) | data formatting | bytes 868352

commit v3 on v2

--- a/solution.py
+++ b/solution.py
@@ -24,7 +24,7 @@
 def step_kernel(
     source, owner, slot, pdf, prior, dissip, react,
     state, les,
-    staged, lhs, onehot, packing, before, part, relay1, got1, relay2, got2,
+    staged, lhs, tall, onehot, packing, before, part, relay1, got1, relay2, got2,
     prior_v, react_v, wide_react, react3, right, ratio, inverse, grown, carried, decayed,
     packed, got_packed, picks, lines, edges, got_edges, ends, got_ends, solved, picked,
     sums, from_twin, relay_b, got_b, total, back, unpacked, gathered,
@@ -88,15 +88,17 @@
     ahead = ((owner[...] & (SIDE - 1)) - x) & (SIDE - 1)
     block = ahead * SIDE + (((owner[...] >> 2) - z) & (SIDE - 1))
 
-    def expand(index, target):
+    relative = (block * cols + slot[...]).astype(jnp.float32)
+    for q in range(cells // 128):
+        at_q = slice(q * 128, (q + 1) * 128)
+        tall[at_q] = jnp.transpose(jnp.broadcast_to(relative[:, at_q], (128, 128)))
+
+    def mark(first, count):
         lane = lax.broadcasted_iota(jnp.int32, (128, 128), 1).astype(jnp.float32)
         for q in range(cells // 128):
-            tall = jnp.transpose(jnp.broadcast_to(index[:, q * 128 : (q + 1) * 128], (128, 128)))
-            for n in range(target.shape[1] // 128):
-                target[q * 128 : (q + 1) * 128, n * 128 : (n + 1) * 128] = bf16_where(tall == lane + float(n * 128))
-
-    expand((block * cols + slot[...]).astype(jnp.float32), onehot)
-    pl.semaphore_wait(barrier, OWNERS - 1 + groups - 1)
+            at_q = slice(q * 128, (q + 1) * 128)
+            for n in range(first, first + count):
+                onehot[at_q, n * 128 : (n + 1) * 128] = bf16_where(tall[at_q] == lane + float(n * 128))
 
     ways_of = ((x_up, x_down, z_up, z_down), (z_up, z_down, x_up, x_down))
 
@@ -130,7 +132,11 @@
         where = c % 2 if isinstance(c, int) else lax.rem(c, 2)
         for k in range(2):
             load(c, rows, where, k).wait()
-        if not isinstance(c, int):
+        if isinstance(c, int):
+            for k in range(2):
+                if c + 1 < STEPS:
+                    load(c + 1, ROWS, 1 - where, k).start()
+        else:
 
             @pl.when(c + 1 < STEPS)
             def full():
@@ -148,6 +154,8 @@
             lhs[(2 + k) * rows : (3 + k) * rows] = low
         trips = [flight(c, rows, k) for k in range(2)]
         for dx in (2, 1, 3, 0):
+            if isinstance(c, int) and c == 0:
+                mark(dx * SIDE, SIDE)
             out = jnp.dot(
                 lhs[0 : 4 * rows], onehot[:, dx * span : (dx + 1) * span], preferred_element_type=jnp.float32
             )
@@ -159,6 +167,8 @@
                         part[trips[0][0], dx, dz, 0:rows] = piece
                     else:
                         part[trips[1][0], dz, dx, 0:rows] = piece
+            if isinstance(c, int) and c == 0 and dx == 2:
+                pl.semaphore_wait(barrier, OWNERS - 1 + groups - 1)
             for m in {2: (0, 1), 1: (2,), 3: (3,), 0: ()}[dx]:
                 trips[0][1](m).start()
         for m in range(4):
@@ -216,13 +226,18 @@
             before[q * 128 : (q + 1) * 128] = bf16_where(rows_ < lax.broadcasted_iota(jnp.int32, (128, cells), 1))
         counts = jnp.dot(bf16_where(mine), before[...], preferred_element_type=jnp.float32)
         rank = jnp.sum(jnp.where(mine, counts, 0.0), axis=0, keepdims=True)
-        expand((block * 128).astype(jnp.float32) + rank, packing)
+        place = (block * 128).astype(jnp.float32) + rank
+        for n in range(OWNERS):
+            packing[n * 128 : (n + 1) * 128] = bf16_where(
+                lax.broadcasted_iota(jnp.int32, (128, cells), 0).astype(jnp.float32) + float(n * 128) == place
+            )
         high, low = split_bf16(pdf[...])
         slots = jnp.broadcast_to(slot[...].astype(jnp.float32), (bins, cells)).astype(jnp.bfloat16)
         for n in range(OWNERS):
             at = slice(n * 128, (n + 1) * 128)
-            out = jnp.dot(
-                jnp.concatenate([high, low, slots], axis=0), packing[:, at], preferred_element_type=jnp.float32
+            out = lax.dot_general(
+                jnp.concatenate([high, low, slots], axis=0), packing[at], (((1,), (1,)), ((), ())),
+                preferred_element_type=jnp.float32,
             )
             packed[n, 0:bins] = out[0:bins] + out[bins : 2 * bins]
             packed[n, bins : bins + 8] = out[2 * bins : 2 * bins + 8]
@@ -300,20 +315,13 @@
 
     def turn(t, carry):
         produce(t, ROWS)
-
-        @pl.when(t >= 1)
-        def _():
-            forward_first(t - 1, ROWS)
+        forward_first(t - 1, ROWS)
 
         @pl.when(t == 1)
         def _():
             pack_weights()
 
-        @pl.when(t == 0)
-        def _():
-            split_react()
-
-        pivots(t * 20, jnp.minimum(t * 20 + 20, every_bin))
+        pivots((t - 1) * 22, jnp.minimum(t * 22, every_bin))
 
         @pl.when(t >= 2)
         def _():
@@ -333,7 +341,9 @@
 
         return carry
 
-    lax.fori_loop(0, STEPS, turn, 0)
+    produce(0, ROWS)
+    split_react()
+    lax.fori_loop(1, STEPS, turn, 0)
     stages = (produce, forward_first, second_stage, forward_second, finish)
     for t in range(STEPS, STEPS + len(stages)):
         for n, stage in enumerate(stages):
@@ -418,15 +428,16 @@
                 sums[j, 2 * n + q] = acc[16 * j : 16 * j + 16]
         return carry
 
-    lax.fori_loop(0, OWNERS // 2, weigh, 0)
-
-    def twin_copy(dy):
-        return remote(sums.at[bin_at(dy, True)], from_twin.at[dy], bin_send, bin_recv, dy, "bin", twin)
-
-    for dy in (2, 1, 3, 0):
-        twin_copy(dy).start()
+    middle = OWNERS // 2
+    parts = (pl.ds(0, middle), pl.ds(middle, middle))
+
+    def twin_copy(dy, h):
+        return remote(
+            sums.at[bin_at(dy, True), parts[h]], from_twin.at[dy, parts[h]], bin_send, bin_recv, 2 * dy + h, "bin", twin
+        )
+
     y_up, y_down = bin_at(1), bin_at(-1)
-    first, rest = pl.ds(0, OWNERS // 2), pl.ds(OWNERS // 2, OWNERS // 2)
+    first, rest = parts
     bin_table = [
         (sums.at[bin_at(2), first], relay_b.at[0], y_up),
         (sums.at[bin_at(2), rest], relay_b.at[1], y_down),
@@ -438,18 +449,29 @@
 
     def bin_copy(m):
         src, dst, who = bin_table[m]
-        return remote(src, dst, bin_send, bin_recv, SIDE + m, "bin", who)
-
-    for dy, then in ((2, (0, 1)), (1, (2,)), (3, (3,)), (0, ())):
-        twin_copy(dy).wait_recv()
-        j = bin_at(dy)
-        sums[j] = sums[j] + from_twin[dy]
-        for m in then:
-            bin_copy(m).start()
-    middle = OWNERS // 2
+        return remote(src, dst, bin_send, bin_recv, 2 * SIDE + m, "bin", who)
+
+    def join_twin(h):
+        for dy, m in ((2, h), (3, 3) if h == 0 else (1, 2), (1, None) if h == 0 else (3, None), (0, None)):
+            twin_copy(dy, h).wait_recv()
+            j = bin_at(dy)
+            at = slice(h * middle, (h + 1) * middle)
+            sums[j, at] = sums[j, at] + from_twin[dy, at]
+            if m is not None:
+                bin_copy(m).start()
+
+    lax.fori_loop(0, 4, weigh, 0)
+    for dy in (2, 3, 1, 0):
+        twin_copy(dy, 0).start()
+    lax.fori_loop(4, 6, weigh, 0)
+    join_twin(0)
+    lax.fori_loop(6, 8, weigh, 0)
+    for dy in (2, 1, 3, 0):
+        twin_copy(dy, 1).start()
     bin_copy(0).wait_recv()
     sums[bin_at(1), 0:middle] = sums[bin_at(1), 0:middle] + relay_b[0]
     bin_copy(4).start()
+    join_twin(1)
     bin_copy(1).wait_recv()
     sums[bin_at(3), middle:OWNERS] = sums[bin_at(3), middle:OWNERS] + relay_b[1]
     bin_copy(5).start()
@@ -464,16 +486,19 @@
     for n in range(1, OWNERS):
         back_copy(n).start()
     back[0] = total[0]
-    for n in range(OWNERS):
-        if n:
-            back_copy(n).wait_recv()
-        high, low = split_bf16(back[n])
-        unpacked[0:16, n * 128 : (n + 1) * 128] = high
-        unpacked[16:32, n * 128 : (n + 1) * 128] = low
-    out = lax.dot_general(
-        unpacked[...], packing[...], (((1,), (1,)), ((), ())), preferred_element_type=jnp.float32
-    )
-    gathered[bin_] = out[0:16] + out[16:32]
+    mine_sum = jnp.zeros((32, cells), jnp.float32)
+    for dx in range(SIDE):
+        for dz in range(SIDE):
+            n = dx * SIDE + dz
+            if n:
+                back_copy(n).wait_recv()
+            high, low = split_bf16(back[n])
+            unpacked[dx, 0:16, dz * 128 : (dz + 1) * 128] = high
+            unpacked[dx, 16:32, dz * 128 : (dz + 1) * 128] = low
+        mine_sum = mine_sum + jnp.dot(
+            unpacked[dx], packing[dx * SIDE * 128 : (dx + 1) * SIDE * 128], preferred_element_type=jnp.float32
+        )
+    gathered[bin_] = mine_sum[0:16] + mine_sum[16:32]
 
     behind, ahead_, across = bin_at(-1), bin_at(1), bin_at(2)
     top, bottom = pl.ds(0, 8), pl.ds(8, 8)
@@ -531,7 +556,8 @@
         edge_copy(d).wait_send()
         end_copy(d).wait_send()
     for dy in range(SIDE):
-        twin_copy(dy).wait_send()
+        for h in range(2):
+            twin_copy(dy, h).wait_send()
     for m in range(6):
         bin_copy(m).wait_send()
     for m in range(8):
@@ -558,8 +584,9 @@
         scratch_shapes=[
             pltpu.VMEM((2, 2, ROWS, cells), f32),
             pltpu.VMEM((4 * ROWS, cells), bf16),
+            pltpu.VMEM((cells, 128), f32),
             pltpu.VMEM((cells, OWNERS * cols), bf16),
-            pltpu.VMEM((cells, OWNERS * 128), bf16),
+            pltpu.VMEM((OWNERS * 128, cells), bf16),
             pltpu.VMEM((cells, cells), bf16),
             pltpu.VMEM((chunks, SIDE, SIDE, ROWS, cols), f32),
             pltpu.VMEM((chunks, 2, 2, ROWS, cols), f32),
@@ -592,7 +619,7 @@
             pltpu.VMEM((2, OWNERS, 16, 128), f32),
             pltpu.VMEM((OWNERS, 16, 128), f32),
             pltpu.VMEM((OWNERS, 16, 128), f32),
-            pltpu.VMEM((32, OWNERS * 128), bf16),
+            pltpu.VMEM((SIDE, 32, SIDE * 128), bf16),
             pltpu.VMEM((groups, 16, cells), f32),
             dma((3, 2)),
             dma((chunks, 12)),
@@ -603,8 +630,8 @@
             dma((groups,)),
             dma((groups,)),
             dma((groups,)),
-            dma((SIDE + 6,)),
-            dma((SIDE + 6,)),
+            dma((2 * SIDE + 6,)),
+            dma((2 * SIDE + 6,)),
             dma((OWNERS,)),
             dma((OWNERS,)),
             dma((8,)),

time: 136 us -> 137 us (level)
  no operation moved by 1% of the time
where the time goes in v3:
time: 137 us
  Pallas kernels  132 us (96%)
  local copies, waits for them, and re-layouts  3.95 us (3%)
    pallas_call x1, Pallas kernels, local(): pl.pallas_call(step_kernel, out_shape=(jax.ShapeDtypeStruct((rows, cols),...  132 us
    unnamed x2, local copies, waits for them, and re-layouts  3.95 us

profile of v3, /device:TPU:1, one launch (start us, length us, event | category | flops | bytes accessed | tf_op | source)
XLA Modules:
  0.0 136.8 jit_solution(15167512177361241971)
XLA Ops:
  0.6 132.2 %cmc_step.1 = (f32[1696,128]{1,0:T(8,128)}, f32[106,1024]{1,0:T(8,128)}) custom-call(f32[1696,1024]{1,0:T(8,128)} %bitcast.15, s32[1,1024]{1,0:T(1,128)} %bitcast.19, s32[1,1024]{1,0:T(1,128)} %bitcast.20, f32[16,1024]{1,0:T(8,128)} %pdf.1, f32[1696,128]{1,0:T(8,128)} %bitcast.16, f32[1,128]{1,0:T(1,128)} %bitcast.21, f32[1696,106]{1,0:T(8,128)} %bitcast.17), custom_call_target="tpu_custom_call" | custom-call | tf_op jit(solution)/shard_map/cmc_step/pallas_call | solution.py:579
  132.8 2.1 %copy.11 = f32[16,106,128]{2,0,1:T(8,128)} copy(f32[16,106,128]{2,0,1:T(8,128)} %bitcast.18) | data formatting | bytes 1736704
  135.0 1.8 %copy.12 = f32[106,1024]{1,0:T(8,128)} copy(f32[106,1024]{1,0:T(8,128)} %get-tuple-element.9) | data formatting | bytes 868352

commit v4 on v3

--- a/solution.py
+++ b/solution.py
@@ -503,46 +503,34 @@
     behind, ahead_, across = bin_at(-1), bin_at(1), bin_at(2)
     top, bottom = pl.ds(0, 8), pl.ds(8, 8)
 
+    near = (bin_at(1), bin_at(1, True), bin_at(-1), bin_at(-1, True), twin)
+    halves = (top, bottom)
+
     def all_copy(m):
-        block_of, part_of, who = [
-            (bin_, None, y_up),
-            (bin_, None, y_down),
-            (bin_, None, twin),
-            (behind, top, y_up),
-            (ahead_, bottom, y_down),
-            (behind, None, twin),
-            (ahead_, None, twin),
-            (across, None, twin),
-        ][m]
-        ref = gathered.at[block_of] if part_of is None else gathered.at[block_of, part_of]
+        if m < 5:
+            ref, who = gathered.at[bin_], near[m]
+        else:
+            up = m < 7
+            ref = gathered.at[behind if up else ahead_, top if up else bottom]
+            who = near[m - 5]
         return remote(ref, ref, all_send, all_recv, m, "bin", who)
 
     def all_arrived(m):
-        block_of, part_of = [
-            (behind, None),
-            (ahead_, None),
-            (twin, None),
-            (across, top),
-            (across, bottom),
-            (bin_at(-1, True), None),
-            (bin_at(1, True), None),
-            (bin_at(2, True), None),
-        ][m]
-        ref = gathered.at[block_of] if part_of is None else gathered.at[block_of, part_of]
+        if m < 5:
+            ref = gathered.at[(bin_at(-1), bin_at(-1, True), bin_at(1), bin_at(1, True), twin)[m]]
+        else:
+            ref = gathered.at[bin_at(2, m % 2 == 0), halves[0] if m < 7 else halves[1]]
         return remote(ref, ref, all_send, all_recv, m, "bin", twin)
 
-    for m in (0, 1, 2):
+    for m in range(5):
         all_copy(m).start()
     all_arrived(0).wait_recv()
-    all_copy(3).start()
-    all_copy(5).start()
-    all_arrived(1).wait_recv()
-    all_copy(4).start()
-    all_copy(6).start()
-    all_arrived(3).wait_recv()
-    all_arrived(4).wait_recv()
-    all_copy(7).start()
-    for m in (2, 5, 6, 7):
+    for m in (5, 6):
+        all_copy(m).start()
+    all_arrived(2).wait_recv()
+    for m in (7, 8):
+        all_copy(m).start()
+    for m in (1, 3, 4, 5, 6, 7, 8):
         all_arrived(m).wait_recv()
     for j in range(groups):
         count = min(16, species - 16 * j)
@@ -560,8 +548,17 @@
             twin_copy(dy, h).wait_send()
     for m in range(6):
         bin_copy(m).wait_send()
-    for m in range(8):
+    for m in range(9):
         all_copy(m).wait_send()
+
+
+def hand_over(state, les, state_out, les_out, sem):
+    pairs = ((state, state_out), (les, les_out))
+    copies = [pltpu.make_async_copy(src, dst, sem.at[n]) for n, (src, dst) in enumerate(pairs)]
+    for copy in copies:
+        copy.start()
+    for copy in copies:
+        copy.wait()
 
 
 def local(les_source, cell_owner, cell_slot, pdf_weight, prior_state, dissip, react_inverse):
@@ -634,8 +631,8 @@
             dma((2 * SIDE + 6,)),
             dma((OWNERS,)),
             dma((OWNERS,)),
-            dma((8,)),
-            dma((8,)),
+            dma((9,)),
+            dma((9,)),
         ],
         compiler_params=pltpu.CompilerParams(collective_id=0, has_side_effects=True, vmem_limit_bytes=63 << 20),
         name="cmc_step",
@@ -648,6 +645,14 @@
         dissip.reshape(1, cols),
         by_species(react_inverse),
     )
+    state, les = pl.pallas_call(
+        hand_over,
+        out_shape=(jax.ShapeDtypeStruct(state.shape, f32), jax.ShapeDtypeStruct(les.shape, f32)),
+        in_specs=[hbm, hbm],
+        out_specs=(hbm, hbm),
+        scratch_shapes=[dma((2,))],
+        name="hand_over",
+    )(state, les)
     return jnp.transpose(state.reshape(species, bins, cols), (1, 0, 2)), les
 
 

time: 137 us -> 173 us (1.26)
  Pallas kernels: 132 us -> 172 us
  local copies, waits for them, and re-layouts: 3.95 us -> 0 us
    pallas_call x0 -> x1, Pallas kernels: none -> 41.3 us  [local(): pl.pallas_call(hand_over, out_shape=(jax.ShapeDtypeStruct(state.shape, f3...]
    unnamed x2 -> x0, local copies, waits for them, and re-layouts: 3.95 us -> none
where the time goes in v4:
time: 173 us
  Pallas kernels  172 us (99%)
    pallas_call x1, Pallas kernels, local(): pl.pallas_call(step_kernel, out_shape=(jax.ShapeDtypeStruct((rows, cols),...  131 us
    pallas_call x1, Pallas kernels, local(): pl.pallas_call(hand_over, out_shape=(jax.ShapeDtypeStruct(state.shape, f3...  41.3 us

profile of v4, /device:TPU:1, one launch (start us, length us, event | category | flops | bytes accessed | tf_op | source)
XLA Modules:
  0.0 173.3 jit_solution(366503890431948154)
XLA Ops:
  0.6 131.1 %cmc_step.1 = (f32[1696,128]{1,0:T(8,128)}, f32[106,1024]{1,0:T(8,128)}) custom-call(f32[1696,1024]{1,0:T(8,128)} %bitcast.15, s32[1,1024]{1,0:T(1,128)} %bitcast.18, s32[1,1024]{1,0:T(1,128)} %bitcast.19, f32[16,1024]{1,0:T(8,128)} %pdf.1, f32[1696,128]{1,0:T(8,128)} %bitcast.16, f32[1,128]{1,0:T(1,128)} %bitcast.20, f32[1696,106]{1,0:T(8,128)} %bitcast.17), custom_call_target="tpu_custom_call" | custom-call | tf_op jit(solution)/shard_map/cmc_step/pallas_call | solution.py:576
  131.8 41.3 %hand_over.1 = (f32[1696,128]{1,0:T(8,128)}, f32[106,1024]{1,0:T(8,128)}) custom-call(f32[1696,128]{1,0:T(8,128)} %get-tuple-element.6.state, f32[106,1024]{1,0:T(8,128)} %get-tuple-element.7.les), custom_call_target="tpu_custom_call" | custom-call | tf_op jit(solution)/shard_map/hand_over/pallas_call | solution.py:648

commit v5 on v4

--- a/solution.py
+++ b/solution.py
@@ -552,13 +552,9 @@
         all_copy(m).wait_send()
 
 
-def hand_over(state, les, state_out, les_out, sem):
-    pairs = ((state, state_out), (les, les_out))
-    copies = [pltpu.make_async_copy(src, dst, sem.at[n]) for n, (src, dst) in enumerate(pairs)]
-    for copy in copies:
-        copy.start()
-    for copy in copies:
-        copy.wait()
+def hand_over(state, les, state_out, les_out):
+    state_out[...] = state[...]
+    les_out[...] = les[...]
 
 
 def local(les_source, cell_owner, cell_slot, pdf_weight, prior_state, dissip, react_inverse):
@@ -648,9 +644,9 @@
     state, les = pl.pallas_call(
         hand_over,
         out_shape=(jax.ShapeDtypeStruct(state.shape, f32), jax.ShapeDtypeStruct(les.shape, f32)),
-        in_specs=[hbm, hbm],
-        out_specs=(hbm, hbm),
-        scratch_shapes=[dma((2,))],
+        in_specs=[vmem, vmem],
+        out_specs=(vmem, vmem),
+        compiler_params=pltpu.CompilerParams(vmem_limit_bytes=8 << 20),
         name="hand_over",
     )(state, les)
     return jnp.transpose(state.reshape(species, bins, cols), (1, 0, 2)), les

time: 173 us -> 135 us (0.78)
  Pallas kernels: 172 us -> 132 us
  local copies, waits for them, and re-layouts: 0 us -> 2.17 us
    pallas_call x1, Pallas kernels: 41.3 us -> 1.14 us  [local(): pl.pallas_call(hand_over, out_shape=(jax.ShapeDtypeStruct(state.shape, f3...]
    unnamed x0 -> x4, local copies, waits for them, and re-layouts: none -> 2.17 us
where the time goes in v5:
time: 135 us
  Pallas kernels  132 us (98%)
  local copies, waits for them, and re-layouts  2.17 us (2%)
    pallas_call x1, Pallas kernels, local(): pl.pallas_call(step_kernel, out_shape=(jax.ShapeDtypeStruct((rows, cols),...  131 us

profile of v5, /device:TPU:1, one launch (start us, length us, event | category | flops | bytes accessed | tf_op | source)
XLA Modules:
  0.0 135.1 jit_solution(13627796973243239359)
XLA Ops:
  0.6 131.1 %cmc_step.1 = (f32[1696,128]{1,0:T(8,128)}, f32[106,1024]{1,0:T(8,128)}) custom-call(f32[1696,1024]{1,0:T(8,128)} %bitcast.15, s32[1,1024]{1,0:T(1,128)} %bitcast.18, s32[1,1024]{1,0:T(1,128)} %bitcast.19, f32[16,1024]{1,0:T(8,128)} %pdf.1, f32[1696,128]{1,0:T(8,128)} %bitcast.16, f32[1,128]{1,0:T(1,128)} %bitcast.20, f32[1696,106]{1,0:T(8,128)} %bitcast.17), custom_call_target="tpu_custom_call" | custom-call | tf_op jit(solution)/shard_map/cmc_step/pallas_call | solution.py:572
  131.8 0.0 copy-start
  131.8 1.2 copy-done
  132.9 0.0 copy-start.1
  133.0 1.0 copy-done.1
  134.0 1.1 hand_over.1
Async XLA Ops:
  131.8 1.2 copy-start
  132.9 1.0 copy-start.1
